TPU v7x, 32 devices: a whole 2x2x4 slice. The times are simulated.
32 devices in a mesh: shard: 4 (over z), tensor: 2 (over y), section: 4 (over x, core).
Axes of the slice: x: 2, y: 2, z: 4, core: 2. Of those that a mesh axis runs over, the one named last changes fastest.
Arguments:
- qkv_grad: bfloat16 [4, 4096, 6144], P('shard', 'section', 'tensor'), may hold values from -150 to 150
- master: float32 [4096, 6144], P(('section', 'shard', 'tensor')), may hold values from -3 to 3
- moment_one: float32 [4096, 6144], P(('section', 'shard', 'tensor')), may hold values from -3 to 3
- moment_two: float32 [4096, 6144], P(('section', 'shard', 'tensor')), may hold values from 0.05 to 2
- average: float32 [4096, 6144], P(('section', 'shard'), 'tensor'), may hold values from -3 to 3
- step: int32 [], replicated, may hold values from 1 to 20
Outputs:
- weights: bfloat16 [4096, 6144], P('section', 'tensor')
- new_master: float32 [4096, 6144], P(('section', 'shard', 'tensor'))
- new_one: float32 [4096, 6144], P(('section', 'shard', 'tensor'))
- new_two: float32 [4096, 6144], P(('section', 'shard', 'tensor'))
- new_average: float32 [4096, 6144], P(('section', 'shard'), 'tensor')
All inputs are finite; a program needn't handle non-finite values.
Results may differ from a plain program's by a relative error of at most 0.0035.
Values may be sent and summed in bfloat16 or wider, within the bound.
A program may use at most 128 MiB of HBM per device.

v0:
```python
import math

import jax
import jax.numpy as jnp
from jax import lax
from jax.sharding import PartitionSpec as P

D = 4096
QKV = 6144


def body(qkv_grad, master, moment_one, moment_two, average, step):
    partial_value = qkv_grad[0]
    shares = lax.psum_scatter(
        partial_value.astype(jnp.float32).astype(jnp.bfloat16),
        "shard",
        scatter_dimension=0,
        tiled=True,
    ).astype(jnp.float32)
    local_sq = jnp.sum(shares * shares)
    grad = lax.all_to_all(
        shares.astype(jnp.bfloat16), "tensor", split_axis=0, concat_axis=1, tiled=True
    ).astype(shares.dtype)
    sumsq = lax.psum(local_sq, ("shard", "tensor", "section"))
    limit = jnp.float32(math.sqrt(D * QKV))
    clip = jnp.minimum(jnp.float32(1.0), limit / (jnp.sqrt(sumsq) + 1e-06))
    clipped = clip * grad
    new_one = 0.9 * moment_one + 0.1 * clipped
    new_two = 0.95 * moment_two + 0.05 * clipped * clipped
    count = step.astype(jnp.float32)
    first_fix = 1.0 - jnp.power(jnp.float32(0.9), count)
    second_fix = 1.0 - jnp.power(jnp.float32(0.95), count)
    update = new_one / first_fix / (jnp.sqrt(new_two / second_fix) + 1e-08)
    new_master = master * (1.0 - 0.1 * 0.1) - 0.1 * update
    returned = lax.all_to_all(
        new_master.astype(jnp.bfloat16), "tensor", split_axis=1, concat_axis=0, tiled=True
    ).astype(new_master.dtype)
    new_average = 0.99 * average + 0.01 * returned
    weights = lax.all_gather(returned.astype(jnp.bfloat16), "shard", axis=0, tiled=True)
    return (weights, new_master, new_one, new_two, new_average)


def solution(mesh):
    in_specs = (
        P("shard", "section", "tensor"),
        P(("section", "shard", "tensor"), None),
        P(("section", "shard", "tensor"), None),
        P(("section", "shard", "tensor"), None),
        P(("section", "shard"), "tensor"),
        P(),
    )
    out_specs = (
        P("section", "tensor"),
        P(("section", "shard", "tensor"), None),
        P(("section", "shard", "tensor"), None),
        P(("section", "shard", "tensor"), None),
        P(("section", "shard"), "tensor"),
    )
    return jax.shard_map(body, mesh=mesh, in_specs=in_specs, out_specs=out_specs, check_vma=False)
```

profile of v0, /device:TPU:0, one launch (start us, length us, event | category | flops | bytes accessed | tf_op | source)
XLA Modules:
  0.0 344.5 jit_solution(15641096911565584398)
XLA Ops:
  7.2 0.0 reduce-scatter.2.cloned.1.call-start
  7.2 0.7 reduce-scatter.2.cloned.1.call-update
  7.9 115.9 %reduce-scatter.2.cloned.1.call-done = bf16[256,3072]{1,0:T(8,128)(2,1)} async-done(((bf16[1024,3072]{1,0:T(8,128)(2,1)}), bf16[256,3072]{1,0:T(8,128)(2,1)}) %reduce-scatter.2.cloned.1.call-update) | async-done | bytes 1572880 | tf_op jit(solution)/shard_map/reduce_scatter | solution.py:14
  123.8 4.6 %all-to-all-start = ((bf16[2,128,3072]{2,1,0:T(8,128)(2,1)}), bf16[2,128,3072]{2,1,0:T(8,128)(2,1)}, u32[]{:S(2)}, u32[]{:S(2)}) async-start(bf16[2,128,3072]{2,1,0:T(8,128)(2,1)} %bitcast.17), calls=%async_computation.1 | async-start | bytes 3145728 | tf_op jit(solution)/shard_map/all_to_all | solution.py:21
  128.4 0.0 all-gather.2.cloned.1.call-start
  129.2 2.4 copy.14
  131.6 3.5 %copy.15 = f32[128,6144]{0,1:T(8,128)} copy(f32[128,6144]{1,0:T(8,128)} %param.8) | data formatting | bytes 6291456 | tf_op args[2]
  135.1 2.8 multiply_reduce_fusion
  137.9 3.5 %copy.17 = f32[128,6144]{0,1:T(8,128)} copy(f32[128,6144]{1,0:T(8,128)} %param.9) | data formatting | bytes 6291456 | tf_op args[3]
  141.5 41.4 %psum.7 = f32[]{:T(128)} all-reduce(f32[]{:T(128)} %multiply_reduce_fusion), channel_id=1, replica_groups=mesh['shard'=4,'tensor'=2,'section'=4] {'shard','tensor','section'}, use_global_device_ids=true, to_apply=%region_2.0 | all-reduce | flops 1 | bytes 8 | tf_op jit(solution)/shard_map/psum | solution.py:24
  183.6 0.0 all-to-all-done
  183.6 2.6 copy.16
  186.2 0.0 copy-start.1
  186.2 1.8 convert_multiply_fusion
  188.0 0.6 copy-done.1
  188.6 5.9 %fusion.2 = (bf16[128,6144]{0,1:T(8,128)(2,1)S(1)}, f32[128,6144]{0,1:T(8,128)}, f32[128,6144]{0,1:T(8,128)}, f32[128,6144]{0,1:T(8,128)}) fusion(f32[]{:T(128)S(6)} %sub.10, f32[]{:T(128)S(6)} %sub.9, f32[128,6144]{0,1:T(8,128)S(1)} %copy.14, f32[2,128,3072]{1,2,0:T(8,128)S(1)} %convert_multiply_fusion, f32[128,6144]{0,1:T(8,128)} %copy.17, ...), kind=kLoop, calls=%fused_computation.8 | loop fusion | flops 11796480 | bytes 23592968 | tf_op jit(solution)/shard_map/convert_element_type | solution.py:36
  194.4 21.4 %all_to_all.32 = bf16[128,2,3072]{0,2,1:T(8,128)(2,1)S(1)} all-to-all(bf16[128,2,3072]{0,2,1:T(8,128)(2,1)S(1)} %bitcast.18), channel_id=1, replica_groups=mesh['shard'=4,'tensor'=2,'section'=4] {'tensor'}, dimensions={1} | all-to-all | bytes 3145728 | tf_op jit(solution)/shard_map/all_to_all | solution.py:35
  215.8 1.6 copy.18
  217.3 0.0 all-gather.2.cloned.1.call-update
  217.4 0.0 copy-start.2
  217.4 3.7 %copy.19 = f32[128,6144]{1,0:T(8,128)} copy(f32[128,6144]{0,1:T(8,128)} %get-tuple-element.11) | data formatting | bytes 6291456
  221.1 0.0 copy-done.2
  221.1 2.4 copy.21
  223.4 0.0 copy-start
  223.4 4.0 %copy.20 = f32[128,6144]{1,0:T(8,128)} copy(f32[128,6144]{0,1:T(8,128)} %get-tuple-element.13) | data formatting | bytes 6291456
  227.5 0.0 copy-done
  227.5 4.3 %multiply_add_fusion = f32[256,3072]{1,0:T(8,128)} fusion(f32[256,3072]{1,0:T(8,128)} %param.10, bf16[2,128,3072]{2,1,0:T(8,128)(2,1)S(1)} %copy-done), kind=kLoop, calls=%fused_computation.4 | loop fusion | flops 3145728 | bytes 7864320 | tf_op jit(solution)/shard_map/add | solution.py:38
  231.8 99.9 %all-gather.2.cloned.1.call-done = bf16[1024,3072]{1,0:T(8,128)(2,1)} async-done(((bf16[256,3072]{1,0:T(8,128)(2,1)}), bf16[1024,3072]{1,0:T(8,128)(2,1)}) %all-gather.2.cloned.1.call-update) | async-done | bytes 6291472 | tf_op jit(solution)/shard_map/all_gather | solution.py:39
  331.7 5.9 %copy.24 = bf16[1024,3072]{1,0:T(8,128)(2,1)} copy(bf16[1024,3072]{1,0:T(8,128)(2,1)} %all-gather.2.cloned.1.call-done) | data formatting | bytes 12582912
Async XLA Ops:
  7.2 116.6 %reduce-scatter.2.cloned.1.call-start = ((), (), s32[]{:S(2)}) async-start(), calls=%async_computation.3 | async-start | bytes 7864320 | tf_op jit(solution)/shard_map/reduce_scatter | solution.py:14
  123.8 59.8 %all-to-all-start = ((bf16[2,128,3072]{2,1,0:T(8,128)(2,1)}), bf16[2,128,3072]{2,1,0:T(8,128)(2,1)}, u32[]{:S(2)}, u32[]{:S(2)}) async-start(bf16[2,128,3072]{2,1,0:T(8,128)(2,1)} %bitcast.17), calls=%async_computation.1 | async-start | bytes 3145728 | tf_op jit(solution)/shard_map/all_to_all | solution.py:21
  128.4 203.3 %all-gather.2.cloned.1.call-start = ((), (), s32[]{:S(2)}) async-start(), calls=%async_computation.4 | async-start | bytes 7864320 | tf_op jit(solution)/shard_map/all_gather | solution.py:39
  186.2 2.4 copy-start.1
  217.4 3.7 %copy-start.2 = (f32[128,6144]{0,1:T(8,128)S(1)}, f32[128,6144]{0,1:T(8,128)}, u32[]{:S(2)}) copy-start(f32[128,6144]{0,1:T(8,128)} %get-tuple-element.12) | copy-start | bytes 9437188
  223.4 4.1 %copy-start = (bf16[2,128,3072]{2,1,0:T(8,128)(2,1)S(1)}, bf16[2,128,3072]{2,1,0:T(8,128)(2,1)}, u32[]{:S(2)}) copy-start(bf16[2,128,3072]{2,1,0:T(8,128)(2,1)} %copy.18) | copy-start | bytes 4718596
Sparse Core Ops, SparseCore 0:
  10.3 113.4 reduce-scatter.1
  217.5 114.2 all-gather.1
where the time goes:
time: 345 us
  waiting for transfers between devices  217 us (63%)
  blocking collectives  62.8 us (18%)
  local copies, waits for them, and re-layouts  30.2 us (9%)
  between operations  15.5 us (4%)
  other arithmetic  14.8 us (4%)
  starting transfers between devices  4.69 us (1%)
    reduce_scatter x1, waiting for transfers between devices, body(): lax.psum_scatter(partial_value.astype(jnp.float32).astype(jnp.bfloat16),...  116 us
    all_gather x1, waiting for transfers between devices, body(): lax.all_gather(returned.astype(jnp.bfloat16), 'shard', axis=0, tiled=True)  99.9 us
    psum x1, blocking collectives, body(): sumsq = lax.psum(local_sq, ('shard', 'tensor', 'section'))  41.4 us
    unnamed x13, local copies, waits for them, and re-layouts  26.1 us
    all_to_all x1, blocking collectives, body(): lax.all_to_all(new_master.astype(jnp.bfloat16), 'tensor', split_axis=1, c...  21.4 us
  transfers between devices with their start and end apart: 3, of which 2 were waited for; matrix products, arithmetic and copies ran while one was open for 8% of the time, Pallas kernels for 0%

commit v1 on v0

v1 whole, which is shorter than its diff:
```python
import functools
import math

import jax
import jax.numpy as jnp
from jax import lax
from jax.experimental import pallas as pl
from jax.experimental.pallas import tpu as pltpu
from jax.sharding import PartitionSpec as P

D = 4096
QKV = 6144


def update_kernel(pos, scal, grad, master, one, two, out_master, out_one, out_two, out_half):
    clip, first_fix, second_fix = scal[0], scal[1], scal[2]
    clipped = clip * grad[0].astype(jnp.float32)
    new_one = 0.9 * one[...] + 0.1 * clipped
    new_two = 0.95 * two[...] + 0.05 * clipped * clipped
    update = new_one / first_fix / (jnp.sqrt(new_two / second_fix) + 1e-08)
    new_master = master[...] * (1.0 - 0.1 * 0.1) - 0.1 * update
    out_one[...] = new_one
    out_two[...] = new_two
    out_master[...] = new_master
    out_half[0] = new_master.astype(jnp.bfloat16)


def update(pos, scal, grads, master, one, two):
    groups, rows, cols = grads.shape
    tile = min(rows, 32)
    state = pl.BlockSpec((tile, cols), lambda k, r, p: (r, lax.rem(p[0] - k + groups, groups)))
    piece = pl.BlockSpec((1, tile, cols), lambda k, r, p: (k, r, 0))
    return pl.pallas_call(
        update_kernel,
        grid_spec=pltpu.PrefetchScalarGridSpec(
            num_scalar_prefetch=1,
            grid=(groups, rows // tile),
            in_specs=[pl.BlockSpec(memory_space=pltpu.SMEM), piece, state, state, state],
            out_specs=[state, state, state, piece],
        ),
        out_shape=[jax.ShapeDtypeStruct(master.shape, jnp.float32)] * 3
        + [jax.ShapeDtypeStruct(grads.shape, jnp.bfloat16)],
        compiler_params=pltpu.CompilerParams(vmem_limit_bytes=32 * 2**20),
        cost_estimate=pl.CostEstimate(flops=master.size * 16, bytes_accessed=master.size * 28, transcendentals=0),
    )(pos, scal, grads, master, one, two)


def place_kernel(pos, piece, *refs):
    refs[-1][...] = piece[...].reshape(refs[-1].shape)


def place(pos, piece, groups, k, held):
    blocks, rows, cols = piece.shape
    in_specs = [pl.BlockSpec((1, rows, cols), lambda s, p: (s, 0, 0))]
    args = [piece]
    aliases = {}
    if held is not None:
        in_specs.append(pl.BlockSpec(memory_space=pl.ANY))
        args.append(held)
        aliases = {2: 0}
    return pl.pallas_call(
        place_kernel,
        grid_spec=pltpu.PrefetchScalarGridSpec(
            num_scalar_prefetch=1,
            grid=(blocks,),
            in_specs=in_specs,
            out_specs=pl.BlockSpec((1, 1, rows, cols), lambda s, p: (s, lax.rem(p[0] + k, groups), 0, 0)),
        ),
        out_shape=jax.ShapeDtypeStruct((blocks, groups, rows, cols), piece.dtype),
        input_output_aliases=aliases,
        cost_estimate=pl.CostEstimate(flops=0, bytes_accessed=piece.size * 4, transcendentals=0),
    )(pos, *args)


def average_kernel(pos, fresh, average, *refs):
    refs[-1][...] = 0.99 * average[...] + 0.01 * fresh[...].astype(jnp.float32)


def average_step(pos, fresh, average, groups, k, held):
    rows, cols = fresh.shape
    block = pl.BlockSpec((rows, cols), lambda i, p: (lax.rem(p[0] + k, groups), 0))
    in_specs = [pl.BlockSpec((rows, cols), lambda i, p: (0, 0)), block]
    args = [fresh, average]
    aliases = {}
    if held is not None:
        in_specs.append(pl.BlockSpec(memory_space=pl.ANY))
        args.append(held)
        aliases = {3: 0}
    return pl.pallas_call(
        average_kernel,
        grid_spec=pltpu.PrefetchScalarGridSpec(
            num_scalar_prefetch=1, grid=(1,), in_specs=in_specs, out_specs=block
        ),
        out_shape=jax.ShapeDtypeStruct(average.shape, jnp.float32),
        input_output_aliases=aliases,
        compiler_params=pltpu.CompilerParams(vmem_limit_bytes=32 * 2**20),
        cost_estimate=pl.CostEstimate(flops=fresh.size * 3, bytes_accessed=fresh.size * 10, transcendentals=0),
    )(pos, *args)


def body(shards, groups, qkv_grad, master, moment_one, moment_two, average, step):
    t = lax.axis_index("tensor")
    pos = jnp.reshape(t, (1,)).astype(jnp.int32)
    rows = qkv_grad.shape[1] // (shards * groups)
    cols = qkv_grad.shape[2]
    blocks = qkv_grad.reshape(shards, groups, rows, cols)
    pieces = [None] * groups
    local_sq = jnp.float32(0.0)
    for k in range(groups - 1, -1, -1):
        block = lax.dynamic_index_in_dim(blocks, lax.rem(t + k, groups), 1, keepdims=False)
        share = lax.psum_scatter(
            block.reshape(shards * rows, cols), "shard", scatter_dimension=0, tiled=True
        )
        wide = share.astype(jnp.float32)
        local_sq = local_sq + jnp.sum(wide * wide)
        if k:
            share = lax.ppermute(share, "tensor", [(i, (i + k) % groups) for i in range(groups)])
        pieces[k] = share
    sumsq = lax.psum(local_sq, ("shard", "tensor", "section"))
    limit = jnp.float32(math.sqrt(D * QKV))
    clip = jnp.minimum(jnp.float32(1.0), limit / (jnp.sqrt(sumsq) + 1e-06))
    count = step.astype(jnp.float32)
    first_fix = 1.0 - jnp.power(jnp.float32(0.9), count)
    second_fix = 1.0 - jnp.power(jnp.float32(0.95), count)
    scal = jnp.stack([clip, first_fix, second_fix])
    new_master, new_one, new_two, half = update(
        pos, scal, jnp.stack(pieces), master, moment_one, moment_two
    )
    weights = None
    new_average = None
    for k in range(groups):
        piece = half[k]
        if k:
            piece = lax.ppermute(piece, "tensor", [(i, (i - k) % groups) for i in range(groups)])
        gathered = lax.all_gather(piece, "shard", axis=0, tiled=False)
        new_average = average_step(pos, piece, average, groups, k, new_average)
        weights = place(pos, gathered, groups, k, weights)
    return (weights.reshape(shards * groups * rows, cols), new_master, new_one, new_two, new_average)


def solution(mesh):
    state = P(("section", "shard", "tensor"), None)
    in_specs = (
        P("shard", "section", "tensor"),
        state,
        state,
        state,
        P(("section", "shard"), "tensor"),
        P(),
    )
    out_specs = (
        P("section", "tensor"),
        state,
        state,
        state,
        P(("section", "shard"), "tensor"),
    )
    fn = functools.partial(body, mesh.shape["shard"], mesh.shape["tensor"])
    return jax.shard_map(fn, mesh=mesh, in_specs=in_specs, out_specs=out_specs, check_vma=False)
```

time: 345 us -> 336 us (0.974)
  blocking collectives: 62.8 us -> 40.3 us
  waiting for transfers between devices: 217 us -> 237 us
  Pallas kernels: 0 us -> 18.3 us
  local copies, waits for them, and re-layouts: 30.2 us -> 12.5 us
  other arithmetic: 14.8 us -> 5.88 us
    all_to_all x1 -> x0, blocking collectives: 21.4 us -> none  [body(): lax.all_to_all(new_master.astype(jnp.bfloat16), 'tensor', split_axis=1, c...]
    unnamed x13 -> x10, local copies, waits for them, and re-layouts: 26.1 us -> 4.92 us
    pallas_call x0 -> x5, Pallas kernels: none -> 18.3 us  [the longest x2 8.37 us: place(): pl.pallas_call(place_kernel, grid_spec=pltpu.PrefetchScalarGridSpec(num_s...]
    ppermute x0 -> x2, waiting for transfers between devices: none -> 16.5 us  [the longest x1 16.5 us: body(): lax.ppermute(piece, 'tensor', [(i, (i - k) % groups) for i in range(group...]
    dynamic_slice x0 -> x1, local copies, waits for them, and re-layouts: none -> 6 us  [body(): lax.dynamic_index_in_dim(blocks, lax.rem(t + k, groups), 1, keepdims=False)]
    convert_element_type x1 -> x0, other arithmetic: 5.87 us -> none  [body(): new_master.astype(jnp.bfloat16)]
    reduce_scatter x1 -> x2, waiting for transfers between devices: 116 us -> 121 us  [body(): lax.psum_scatter(block.reshape(shards * rows, cols), 'shard', scatter_dim...]
    all_to_all x1 -> x0, starting transfers between devices: 4.61 us -> none  [body(): lax.all_to_all(shares.astype(jnp.bfloat16), 'tensor', split_axis=0, conca...]
  transfers between devices with their start and end apart: 3 -> 6, of which waited for: 2 -> 5; matrix products, arithmetic and copies ran while one was open for 8% -> 1% of each run, Pallas kernels for 0% -> 2%
where the time goes in v1:
time: 336 us; the launch traced here: 335 us
  waiting for transfers between devices  237 us (71%)
  blocking collectives  40.3 us (12%)
  Pallas kernels  18.3 us (5%)
  between operations  16.6 us (5%)
  local copies, waits for them, and re-layouts  12.5 us (4%)
  other arithmetic  5.88 us (2%)
  starting transfers between devices  4.15 us (1%)
    reduce_scatter x2, waiting for transfers between devices, body(): lax.psum_scatter(block.reshape(shards * rows, cols), 'shard', scatter_dim...  121 us
    all_gather x2, waiting for transfers between devices, body(): gathered = lax.all_gather(piece, 'shard', axis=0, tiled=False)  98.9 us
    psum x1, blocking collectives, body(): sumsq = lax.psum(local_sq, ('shard', 'tensor', 'section'))  40.3 us
    ppermute x1, waiting for transfers between devices, body(): lax.ppermute(piece, 'tensor', [(i, (i - k) % groups) for i in range(group...  16.5 us
    pallas_call x2, Pallas kernels, place(): pl.pallas_call(place_kernel, grid_spec=pltpu.PrefetchScalarGridSpec(num_s...  8.37 us
  transfers between devices with their start and end apart: 6, of which 5 were waited for; matrix products, arithmetic and copies ran while one was open for 1% of the time, Pallas kernels for 2%

profile of v1, /device:TPU:0, one launch (start us, length us, event | category | flops | bytes accessed | tf_op | source)
XLA Modules:
  0.0 335.0 jit_solution(10091950226791254562)
XLA Ops:
  7.2 0.0 reduce-scatter.3.cloned.1.call-start
  7.2 6.0 %constant_dynamic-slice_fusion = (bf16[4,1,128,3072]{3,2,1,0:T(8,128)(2,1)}, bf16[4,1,128,3072]{3,2,1,0:T(8,128)(2,1)}) fusion(bf16[4,2,128,3072]{3,2,1,0:T(8,128)(2,1)} %bitcast.22, s32[]{:T(128)S(6)} %select_n.8, s32[]{:T(128)S(6)} %select_n.7), kind=kLoop, calls=%fused_computation.5 | loop fusion | bytes 12582920 | tf_op jit(solution)/shard_map/jit(dynamic_index_in_dim)/dynamic_slice | solution.py:110
  13.2 0.0 reduce-scatter.3.cloned.1.call-update
  13.2 0.0 reduce-scatter.5.cloned.1.call-start
  13.3 0.7 reduce-scatter.5.cloned.1.call-update
  14.0 0.0 copy-start.1
  14.0 0.0 all-gather.4.cloned.1.call-start
  14.1 62.3 %reduce-scatter.3.cloned.1.call-done = bf16[128,3072]{1,0:T(8,128)(2,1)} async-done(((bf16[512,3072]{1,0:T(8,128)(2,1)}), bf16[128,3072]{1,0:T(8,128)(2,1)}) %reduce-scatter.3.cloned.1.call-update) | async-done | bytes 786448 | tf_op jit(solution)/shard_map/reduce_scatter | solution.py:111
  76.4 1.5 collective-permute-start
  78.6 2.1 multiply_reduce_fusion.1
  80.7 58.8 %reduce-scatter.5.cloned.1.call-done = bf16[128,3072]{1,0:T(8,128)(2,1)} async-done(((bf16[512,3072]{1,0:T(8,128)(2,1)}), bf16[128,3072]{1,0:T(8,128)(2,1)}) %reduce-scatter.5.cloned.1.call-update) | async-done | bytes 786448 | tf_op jit(solution)/shard_map/reduce_scatter | solution.py:111
  139.5 2.1 multiply_reduce_fusion
  143.0 40.3 %psum.7 = f32[]{:T(128)} all-reduce(f32[]{:T(128)S(6)} %add.25), channel_id=1, replica_groups=mesh['shard'=4,'tensor'=2,'section'=4] {'shard','tensor','section'}, use_global_device_ids=true, to_apply=%region_4.5 | all-reduce | flops 1 | bytes 8 | tf_op jit(solution)/shard_map/psum | solution.py:119
  184.0 0.1 pad_maximum_fusion.1.scal
  184.1 1.5 pad_maximum_fusion.grad
  185.6 0.0 copy-start.2
  185.6 1.9 copy-done.2
  187.5 1.9 copy-done.3
  189.4 6.1 %shard_map.101 = (f32[128,6144]{1,0:T(8,128)}, f32[128,6144]{1,0:T(8,128)}, f32[128,6144]{1,0:T(8,128)}, bf16[2,128,3072]{2,1,0:T(8,128)(2,1)S(1)}) custom-call(s32[1]{0:T(128)} %bitcast.pos, f32[3]{0:T(128)S(1)} %pad_maximum_fusion.1.scal, bf16[2,128,3072]{2,1,0:T(8,128)(2,1)S(1)} %pad_maximum_fusion.grad, f32[128,6144]{1,0:T(8,128)S(1)} %copy-done.1, ...), custom_call_target="tpu_custom_call" | custom-call | flops 12582912 | bytes 22020096 | tf_op jit(solution)/shard_map/pallas_call | solution.py:33
  195.5 1.6 slice_bitcast_fusion.1
  197.1 0.0 all-gather.4.cloned.1.call-update
  197.1 0.0 all-gather.6.cloned.1.call-start
  197.1 2.5 collective-permute-start.1
  199.7 16.5 %collective-permute-done.1.fresh = bf16[128,3072]{1,0:T(8,128)(2,1)} collective-permute-done((bf16[128,3072]{1,0:T(8,128)(2,1)}, bf16[128,3072]{1,0:T(8,128)(2,1)}, u32[]{:S(2)}, u32[]{:S(2)}) %collective-permute-start.1) | collective-permute-done | bytes 786464 | tf_op jit(solution)/shard_map/ppermute | solution.py:134
  216.2 0.0 all-gather.6.cloned.1.call-update
  216.2 1.1 copy-done.4
  217.4 1.4 shard_map.104.refs_0_
  218.7 2.5 shard_map.105
  221.2 39.5 %all-gather.4.cloned.1.call-done.piece = bf16[4,128,3072]{2,1,0:T(8,128)(2,1)} async-done(((bf16[1,128,3072]{2,1,0:T(8,128)(2,1)}), bf16[4,128,3072]{2,1,0:T(8,128)(2,1)}) %all-gather.4.cloned.1.call-update) | async-done | bytes 3145744 | tf_op jit(solution)/shard_map/all_gather | solution.py:135
  260.7 4.2 %shard_map.102.refs_0_ = bf16[4,2,128,3072]{3,2,1,0:T(8,128)(2,1)} custom-call(s32[1]{0:T(128)} %bitcast.pos, bf16[4,128,3072]{2,1,0:T(8,128)(2,1)} %all-gather.4.cloned.1.call-done.piece), custom_call_target="tpu_custom_call" | custom-call | bytes 6291456 | tf_op jit(solution)/shard_map/pallas_call | solution.py:61
  264.9 59.4 %all-gather.6.cloned.1.call-done = bf16[512,3072]{1,0:T(8,128)(2,1)} async-done(((bf16[128,3072]{1,0:T(8,128)(2,1)}), bf16[512,3072]{1,0:T(8,128)(2,1)}) %all-gather.6.cloned.1.call-update) | async-done | bytes 3145744 | tf_op jit(solution)/shard_map/all_gather | solution.py:135
  324.3 4.2 %shard_map.103 = bf16[4,2,128,3072]{3,2,1,0:T(8,128)(2,1)} custom-call(s32[1]{0:T(128)} %bitcast.pos, bf16[4,128,3072]{2,1,0:T(8,128)(2,1)} %bitcast.23, bf16[4,2,128,3072]{3,2,1,0:T(8,128)(2,1)} %shard_map.102.refs_0_), custom_call_target="tpu_custom_call", output_to_operand_aliasing={{}: (2, {})} | custom-call | bytes 6291456 | tf_op jit(solution)/shard_map/pallas_call | solution.py:61
  (6 shorter events, 0.0 us)
Async XLA Ops:
  7.2 69.2 %reduce-scatter.3.cloned.1.call-start = ((), (), s32[]{:S(2)}) async-start(), calls=%async_computation.2 | async-start | bytes 3932160 | tf_op jit(solution)/shard_map/reduce_scatter | solution.py:111
  13.2 126.3 %reduce-scatter.5.cloned.1.call-start = ((), (), s32[]{:S(2)}) async-start(), calls=%async_computation.3 | async-start | bytes 3932160 | tf_op jit(solution)/shard_map/reduce_scatter | solution.py:111
  14.0 171.6 %copy-start.1 = (f32[128,6144]{1,0:T(8,128)S(1)}, f32[128,6144]{1,0:T(8,128)}, u32[]{:S(2)}) copy-start(f32[128,6144]{1,0:T(8,128)} %master.1) | copy-start | bytes 9437188
  14.0 246.7 %all-gather.4.cloned.1.call-start = ((), (), s32[]{:S(2)}) async-start(), calls=%async_computation.4 | async-start | bytes 3932160 | tf_op jit(solution)/shard_map/all_gather | solution.py:135
  76.4 107.7 %collective-permute-start = (bf16[128,3072]{1,0:T(8,128)(2,1)}, bf16[128,3072]{1,0:T(8,128)(2,1)}, u32[]{:S(2)}, u32[]{:S(2)}) collective-permute-start(bf16[128,3072]{1,0:T(8,128)(2,1)} %reduce-scatter.3.cloned.1.call-done), channel_id=1, source_target_pairs={{0,4},{4,0},{1,5},{5,1},{2,6},{6,2},{3,7},{7,3},{8,12},{12,8},{9,1... | collective-permute-start | bytes 2359304 | tf_op jit(solution)/shard_map/ppermute | solution.py:117
  185.6 1.9 copy-start.2
  187.5 1.9 copy-start.3
  195.5 20.7 %copy-start = (f32[256,3072]{1,0:T(8,128)S(1)}, f32[256,3072]{1,0:T(8,128)}, u32[]{:S(2)}) copy-start(f32[256,3072]{1,0:T(8,128)} %average.3) | copy-start | bytes 9437188
  197.1 127.2 %all-gather.6.cloned.1.call-start = ((), (), s32[]{:S(2)}) async-start(), calls=%async_computation.5 | async-start | bytes 3932160 | tf_op jit(solution)/shard_map/all_gather | solution.py:135
  197.1 19.0 %collective-permute-start.1 = (bf16[128,3072]{1,0:T(8,128)(2,1)}, bf16[128,3072]{1,0:T(8,128)(2,1)}, u32[]{:S(2)}, u32[]{:S(2)}) collective-permute-start(bf16[128,3072]{1,0:T(8,128)(2,1)} %get-tuple-element.17), channel_id=1, source_target_pairs={{0,4},{4,0},{1,5},{5,1},{2,6},{6,2},{3,7},{7,3},{8,12},{12,8},{9,1... | collective-permute-start | bytes 2359304 | tf_op jit(solution)/shard_map/ppermute | solution.py:134
  216.2 1.1 copy-start.4
Sparse Core Ops, SparseCore 0:
  13.4 62.9 reduce-scatter.2
  79.2 60.2 reduce-scatter.4
  197.2 63.4 all-gather.3
  262.1 62.1 all-gather.5

commit v2 on v1

--- a/solution.py
+++ b/solution.py
@@ -98,7 +98,62 @@
     )(pos, *args)
 
 
-def body(shards, groups, qkv_grad, master, moment_one, moment_two, average, step):
+MESH = pl.DeviceIdType.MESH
+
+
+def total_kernel(axes, x_ref, out_ref, held, send_sem, recv_sem):
+    barrier = pltpu.get_barrier_semaphore()
+    count = 0
+    for name, size in axes:
+        me = lax.axis_index(name)
+        for off in range(1, size):
+            pl.semaphore_signal(
+                barrier, inc=1, device_id={name: lax.rem(me + off, size)}, device_id_type=MESH
+            )
+            count += 1
+    pl.semaphore_wait(barrier, count)
+    at = 0
+    own = x_ref[...]
+    for name, size in axes:
+        me = lax.axis_index(name)
+        held[at] = own
+        copies = []
+        for off in range(1, size):
+            copy = pltpu.make_async_remote_copy(
+                src_ref=held.at[at],
+                dst_ref=held.at[at + off],
+                send_sem=send_sem.at[at + off],
+                recv_sem=recv_sem.at[at + off],
+                device_id={name: lax.rem(me + off, size)},
+                device_id_type=MESH,
+            )
+            copy.start()
+            copies.append(copy)
+        for off, copy in enumerate(copies, 1):
+            copy.wait()
+            own = own + held[at + off]
+        at += size
+    out_ref[...] = own
+
+
+def total(axes, value):
+    slots = sum(size for _, size in axes)
+    return pl.pallas_call(
+        functools.partial(total_kernel, axes),
+        out_shape=jax.ShapeDtypeStruct((8, 128), jnp.float32),
+        in_specs=[pl.BlockSpec(memory_space=pltpu.VMEM)],
+        out_specs=pl.BlockSpec(memory_space=pltpu.VMEM),
+        scratch_shapes=[
+            pltpu.VMEM((slots, 8, 128), jnp.float32),
+            pltpu.SemaphoreType.DMA((slots,)),
+            pltpu.SemaphoreType.DMA((slots,)),
+        ],
+        compiler_params=pltpu.CompilerParams(collective_id=0, has_side_effects=True),
+    )(jnp.full((8, 128), value, jnp.float32))[0, 0]
+
+
+def body(axes, qkv_grad, master, moment_one, moment_two, average, step):
+    shards, groups = dict(axes)["shard"], dict(axes)["tensor"]
     t = lax.axis_index("tensor")
     pos = jnp.reshape(t, (1,)).astype(jnp.int32)
     rows = qkv_grad.shape[1] // (shards * groups)
@@ -116,7 +171,7 @@
         if k:
             share = lax.ppermute(share, "tensor", [(i, (i + k) % groups) for i in range(groups)])
         pieces[k] = share
-    sumsq = lax.psum(local_sq, ("shard", "tensor", "section"))
+    sumsq = total(axes, local_sq)
     limit = jnp.float32(math.sqrt(D * QKV))
     clip = jnp.minimum(jnp.float32(1.0), limit / (jnp.sqrt(sumsq) + 1e-06))
     count = step.astype(jnp.float32)
@@ -155,5 +210,5 @@
         state,
         P(("section", "shard"), "tensor"),
     )
-    fn = functools.partial(body, mesh.shape["shard"], mesh.shape["tensor"])
+    fn = functools.partial(body, [(name, mesh.shape[name]) for name in ("tensor", "section", "shard")])
     return jax.shard_map(fn, mesh=mesh, in_specs=in_specs, out_specs=out_specs, check_vma=False)

time: 336 us -> 309 us (0.920)
  blocking collectives: 40.3 us -> 0 us
  Pallas kernels: 18.3 us -> 31.4 us
    psum x1 -> x0, blocking collectives: 40.3 us -> none  [body(): sumsq = lax.psum(local_sq, ('shard', 'tensor', 'section'))]
    pallas_call x0 -> x1, Pallas kernels: none -> 13.1 us  [total(): pl.pallas_call(functools.partial(total_kernel, axes), out_shape=jax.Shape...]
  transfers between devices with their start and end apart: 6 -> 6, of which waited for: 5 -> 5; matrix products, arithmetic and copies ran while one was open for 1% -> 2% of each run, Pallas kernels for 2% -> 7%
where the time goes in v2:
time: 309 us; the launch traced here: 308 us
  waiting for transfers between devices  237 us (77%)
  Pallas kernels  31.4 us (10%)
  between operations  16.6 us (5%)
  local copies, waits for them, and re-layouts  14.3 us (5%)
  other arithmetic  5.88 us (2%)
    reduce_scatter x2, waiting for transfers between devices, body(): lax.psum_scatter(block.reshape(shards * rows, cols), 'shard', scatter_dim...  121 us
    all_gather x2, waiting for transfers between devices, body(): gathered = lax.all_gather(piece, 'shard', axis=0, tiled=False)  97.1 us
    ppermute x1, waiting for transfers between devices, body(): lax.ppermute(piece, 'tensor', [(i, (i - k) % groups) for i in range(group...  18.4 us
    pallas_call x1, Pallas kernels, total(): pl.pallas_call(functools.partial(total_kernel, axes), out_shape=jax.Shape...  13.1 us
    pallas_call x2, Pallas kernels, place(): pl.pallas_call(place_kernel, grid_spec=pltpu.PrefetchScalarGridSpec(num_s...  8.37 us
  transfers between devices with their start and end apart: 6, of which 5 were waited for; matrix products, arithmetic and copies ran while one was open for 2% of the time, Pallas kernels for 7%

profile of v2, /device:TPU:0, one launch (start us, length us, event | category | flops | bytes accessed | tf_op | source)
XLA Modules:
  0.0 307.9 jit_solution(1461495665764088829)
XLA Ops:
  7.2 0.0 reduce-scatter.3.cloned.1.call-start
  7.2 6.0 %constant_dynamic-slice_fusion = (bf16[4,1,128,3072]{3,2,1,0:T(8,128)(2,1)}, bf16[4,1,128,3072]{3,2,1,0:T(8,128)(2,1)}) fusion(bf16[4,2,128,3072]{3,2,1,0:T(8,128)(2,1)} %bitcast.22, s32[]{:T(128)S(6)} %select_n.8, s32[]{:T(128)S(6)} %select_n.7), kind=kLoop, calls=%fused_computation.5 | loop fusion | bytes 12582920 | tf_op jit(solution)/shard_map/jit(dynamic_index_in_dim)/dynamic_slice | solution.py:165
  13.2 0.0 reduce-scatter.3.cloned.1.call-update
  13.2 0.0 reduce-scatter.5.cloned.1.call-start
  13.3 0.7 reduce-scatter.5.cloned.1.call-update
  14.0 0.0 all-gather.4.cloned.1.call-start
  14.1 62.3 %reduce-scatter.3.cloned.1.call-done = bf16[128,3072]{1,0:T(8,128)(2,1)} async-done(((bf16[512,3072]{1,0:T(8,128)(2,1)}), bf16[128,3072]{1,0:T(8,128)(2,1)}) %reduce-scatter.3.cloned.1.call-update) | async-done | bytes 786448 | tf_op jit(solution)/shard_map/reduce_scatter | solution.py:166
  76.4 1.5 collective-permute-start
  78.6 2.1 multiply_reduce_fusion.1
  80.7 58.8 %reduce-scatter.5.cloned.1.call-done = bf16[128,3072]{1,0:T(8,128)(2,1)} async-done(((bf16[512,3072]{1,0:T(8,128)(2,1)}), bf16[128,3072]{1,0:T(8,128)(2,1)}) %reduce-scatter.5.cloned.1.call-update) | async-done | bytes 786448 | tf_op jit(solution)/shard_map/reduce_scatter | solution.py:166
  139.5 2.1 multiply_reduce_fusion
  143.0 0.6 broadcast_in_dim.3.x_ref
  143.6 13.1 %shard_map.101 = f32[8,128]{1,0:T(8,128)} custom-call(f32[8,128]{1,0:T(8,128)} %broadcast_in_dim.3.x_ref), custom_call_target="tpu_custom_call" | custom-call | tf_op jit(solution)/shard_map/pallas_call | solution.py:141
  156.6 1.2 slice.9
  158.6 0.1 pad_maximum_fusion.1.scal
  158.7 1.5 pad_maximum_fusion.grad
  160.2 1.9 copy-done.2
  162.1 1.9 copy-done.3
  164.0 6.1 %shard_map.102 = (f32[128,6144]{1,0:T(8,128)}, f32[128,6144]{1,0:T(8,128)}, f32[128,6144]{1,0:T(8,128)}, bf16[2,128,3072]{2,1,0:T(8,128)(2,1)S(1)}) custom-call(s32[1]{0:T(128)} %bitcast.pos, f32[3]{0:T(128)S(1)} %pad_maximum_fusion.1.scal, bf16[2,128,3072]{2,1,0:T(8,128)(2,1)S(1)} %pad_maximum_fusion.grad, f32[128,6144]{1,0:T(8,128)S(1)} %copy-done.1, ...), custom_call_target="tpu_custom_call" | custom-call | flops 12582912 | bytes 22020096 | tf_op jit(solution)/shard_map/pallas_call | solution.py:33
  170.1 1.6 slice_bitcast_fusion.1
  171.6 0.0 all-gather.4.cloned.1.call-update
  171.7 0.0 all-gather.6.cloned.1.call-start
  171.7 0.7 collective-permute-start.1
  172.4 18.4 %collective-permute-done.1.fresh = bf16[128,3072]{1,0:T(8,128)(2,1)} collective-permute-done((bf16[128,3072]{1,0:T(8,128)(2,1)}, bf16[128,3072]{1,0:T(8,128)(2,1)}, u32[]{:S(2)}, u32[]{:S(2)}) %collective-permute-start.1) | collective-permute-done | bytes 786464 | tf_op jit(solution)/shard_map/ppermute | solution.py:189
  190.8 0.0 all-gather.6.cloned.1.call-update
  190.8 1.1 copy-done.4
  192.0 1.4 shard_map.105.refs_0_
  193.3 2.5 shard_map.106
  195.8 37.7 %all-gather.4.cloned.1.call-done.piece = bf16[4,128,3072]{2,1,0:T(8,128)(2,1)} async-done(((bf16[1,128,3072]{2,1,0:T(8,128)(2,1)}), bf16[4,128,3072]{2,1,0:T(8,128)(2,1)}) %all-gather.4.cloned.1.call-update) | async-done | bytes 3145744 | tf_op jit(solution)/shard_map/all_gather | solution.py:190
  233.5 4.2 %shard_map.103.refs_0_ = bf16[4,2,128,3072]{3,2,1,0:T(8,128)(2,1)} custom-call(s32[1]{0:T(128)} %bitcast.pos, bf16[4,128,3072]{2,1,0:T(8,128)(2,1)} %all-gather.4.cloned.1.call-done.piece), custom_call_target="tpu_custom_call" | custom-call | bytes 6291456 | tf_op jit(solution)/shard_map/pallas_call | solution.py:61
  237.7 59.4 %all-gather.6.cloned.1.call-done = bf16[512,3072]{1,0:T(8,128)(2,1)} async-done(((bf16[128,3072]{1,0:T(8,128)(2,1)}), bf16[512,3072]{1,0:T(8,128)(2,1)}) %all-gather.6.cloned.1.call-update) | async-done | bytes 3145744 | tf_op jit(solution)/shard_map/all_gather | solution.py:190
  297.1 4.2 %shard_map.104 = bf16[4,2,128,3072]{3,2,1,0:T(8,128)(2,1)} custom-call(s32[1]{0:T(128)} %bitcast.pos, bf16[4,128,3072]{2,1,0:T(8,128)(2,1)} %bitcast.23, bf16[4,2,128,3072]{3,2,1,0:T(8,128)(2,1)} %shard_map.103.refs_0_), custom_call_target="tpu_custom_call", output_to_operand_aliasing={{}: (2, {})} | custom-call | bytes 6291456 | tf_op jit(solution)/shard_map/pallas_call | solution.py:61
  (8 shorter events, 0.0 us)
Async XLA Ops:
  7.2 69.2 %reduce-scatter.3.cloned.1.call-start = ((), (), s32[]{:S(2)}) async-start(), calls=%async_computation.2 | async-start | bytes 3932160 | tf_op jit(solution)/shard_map/reduce_scatter | solution.py:166
  13.2 126.3 %reduce-scatter.5.cloned.1.call-start = ((), (), s32[]{:S(2)}) async-start(), calls=%async_computation.3 | async-start | bytes 3932160 | tf_op jit(solution)/shard_map/reduce_scatter | solution.py:166
  14.0 146.2 %copy-start.1 = (f32[128,6144]{1,0:T(8,128)S(1)}, f32[128,6144]{1,0:T(8,128)}, u32[]{:S(2)}) copy-start(f32[128,6144]{1,0:T(8,128)} %master.1) | copy-start | bytes 9437188
  14.0 219.5 %all-gather.4.cloned.1.call-start = ((), (), s32[]{:S(2)}) async-start(), calls=%async_computation.4 | async-start | bytes 3932160 | tf_op jit(solution)/shard_map/all_gather | solution.py:190
  76.4 82.3 %collective-permute-start = (bf16[128,3072]{1,0:T(8,128)(2,1)}, bf16[128,3072]{1,0:T(8,128)(2,1)}, u32[]{:S(2)}, u32[]{:S(2)}) collective-permute-start(bf16[128,3072]{1,0:T(8,128)(2,1)} %reduce-scatter.3.cloned.1.call-done), channel_id=1, source_target_pairs={{0,4},{4,0},{1,5},{5,1},{2,6},{6,2},{3,7},{7,3},{8,12},{12,8},{9,1... | collective-permute-start | bytes 2359304 | tf_op jit(solution)/shard_map/ppermute | solution.py:172
  160.2 1.9 copy-start.2
  162.1 1.9 copy-start.3
  170.1 20.8 %copy-start = (f32[256,3072]{1,0:T(8,128)S(1)}, f32[256,3072]{1,0:T(8,128)}, u32[]{:S(2)}) copy-start(f32[256,3072]{1,0:T(8,128)} %average.3) | copy-start | bytes 9437188
  171.7 125.5 %all-gather.6.cloned.1.call-start = ((), (), s32[]{:S(2)}) async-start(), calls=%async_computation.5 | async-start | bytes 3932160 | tf_op jit(solution)/shard_map/all_gather | solution.py:190
  171.7 19.1 %collective-permute-start.1 = (bf16[128,3072]{1,0:T(8,128)(2,1)}, bf16[128,3072]{1,0:T(8,128)(2,1)}, u32[]{:S(2)}, u32[]{:S(2)}) collective-permute-start(bf16[128,3072]{1,0:T(8,128)(2,1)} %get-tuple-element.17), channel_id=1, source_target_pairs={{0,4},{4,0},{1,5},{5,1},{2,6},{6,2},{3,7},{7,3},{8,12},{12,8},{9,1... | collective-permute-start | bytes 2359304 | tf_op jit(solution)/shard_map/ppermute | solution.py:189
  190.8 1.1 copy-start.4
Sparse Core Ops, SparseCore 0:
  13.4 62.9 reduce-scatter.2
  79.2 60.2 reduce-scatter.4
  171.8 61.7 all-gather.3
  235.0 62.1 all-gather.5

commit v3 on v2

--- a/solution.py
+++ b/solution.py
@@ -43,59 +43,6 @@
         compiler_params=pltpu.CompilerParams(vmem_limit_bytes=32 * 2**20),
         cost_estimate=pl.CostEstimate(flops=master.size * 16, bytes_accessed=master.size * 28, transcendentals=0),
     )(pos, scal, grads, master, one, two)
-
-
-def place_kernel(pos, piece, *refs):
-    refs[-1][...] = piece[...].reshape(refs[-1].shape)
-
-
-def place(pos, piece, groups, k, held):
-    blocks, rows, cols = piece.shape
-    in_specs = [pl.BlockSpec((1, rows, cols), lambda s, p: (s, 0, 0))]
-    args = [piece]
-    aliases = {}
-    if held is not None:
-        in_specs.append(pl.BlockSpec(memory_space=pl.ANY))
-        args.append(held)
-        aliases = {2: 0}
-    return pl.pallas_call(
-        place_kernel,
-        grid_spec=pltpu.PrefetchScalarGridSpec(
-            num_scalar_prefetch=1,
-            grid=(blocks,),
-            in_specs=in_specs,
-            out_specs=pl.BlockSpec((1, 1, rows, cols), lambda s, p: (s, lax.rem(p[0] + k, groups), 0, 0)),
-        ),
-        out_shape=jax.ShapeDtypeStruct((blocks, groups, rows, cols), piece.dtype),
-        input_output_aliases=aliases,
-        cost_estimate=pl.CostEstimate(flops=0, bytes_accessed=piece.size * 4, transcendentals=0),
-    )(pos, *args)
-
-
-def average_kernel(pos, fresh, average, *refs):
-    refs[-1][...] = 0.99 * average[...] + 0.01 * fresh[...].astype(jnp.float32)
-
-
-def average_step(pos, fresh, average, groups, k, held):
-    rows, cols = fresh.shape
-    block = pl.BlockSpec((rows, cols), lambda i, p: (lax.rem(p[0] + k, groups), 0))
-    in_specs = [pl.BlockSpec((rows, cols), lambda i, p: (0, 0)), block]
-    args = [fresh, average]
-    aliases = {}
-    if held is not None:
-        in_specs.append(pl.BlockSpec(memory_space=pl.ANY))
-        args.append(held)
-        aliases = {3: 0}
-    return pl.pallas_call(
-        average_kernel,
-        grid_spec=pltpu.PrefetchScalarGridSpec(
-            num_scalar_prefetch=1, grid=(1,), in_specs=in_specs, out_specs=block
-        ),
-        out_shape=jax.ShapeDtypeStruct(average.shape, jnp.float32),
-        input_output_aliases=aliases,
-        compiler_params=pltpu.CompilerParams(vmem_limit_bytes=32 * 2**20),
-        cost_estimate=pl.CostEstimate(flops=fresh.size * 3, bytes_accessed=fresh.size * 10, transcendentals=0),
-    )(pos, *args)
 
 
 MESH = pl.DeviceIdType.MESH
@@ -152,6 +99,123 @@
     )(jnp.full((8, 128), value, jnp.float32))[0, 0]
 
 
+def spread_kernel(shards, groups, half, out, y_send, y_recv, z_send, z_recv, own_sem):
+    s = lax.axis_index("shard")
+    t = lax.axis_index("tensor")
+    last = shards - 1
+    barrier = pltpu.get_barrier_semaphore()
+    for off in range(1, groups):
+        pl.semaphore_signal(
+            barrier, inc=1, device_id={"tensor": lax.rem(t + off, groups)}, device_id_type=MESH
+        )
+
+    @pl.when(s < last)
+    def _():
+        pl.semaphore_signal(barrier, inc=1, device_id={"shard": s + 1}, device_id_type=MESH)
+
+    @pl.when(s > 0)
+    def _():
+        pl.semaphore_signal(barrier, inc=1, device_id={"shard": s - 1}, device_id_type=MESH)
+
+    peers = groups - 1 + jnp.minimum(s, 1) + jnp.minimum(last - s, 1)
+    pl.semaphore_wait(barrier, peers)
+
+    def across(k):
+        return pltpu.make_async_remote_copy(
+            src_ref=half.at[k],
+            dst_ref=out.at[s, t],
+            send_sem=y_send.at[k],
+            recv_sem=y_recv.at[k],
+            device_id={"tensor": lax.rem(t - k + groups, groups)},
+            device_id_type=MESH,
+        )
+
+    def hop(way, k, d):
+        slot = s - d if way == 0 else s + d
+        group = lax.rem(t + k, groups)
+        return pltpu.make_async_remote_copy(
+            src_ref=half.at[0] if k == 0 and d == 0 else out.at[slot, group],
+            dst_ref=out.at[slot, group],
+            send_sem=z_send.at[way, k, d],
+            recv_sem=z_recv.at[way, k, d],
+            device_id={"shard": s + 1 if way == 0 else s - 1},
+            device_id_type=MESH,
+        )
+
+    def arrival(way, k, d):
+        slot = s - d if way == 0 else s + d
+        group = lax.rem(t + k, groups)
+        return pltpu.make_async_remote_copy(
+            src_ref=out.at[slot, group],
+            dst_ref=out.at[slot, group],
+            send_sem=z_send.at[way, k, d - 1],
+            recv_sem=z_recv.at[way, k, d - 1],
+            device_id={"shard": s - 1 if way == 0 else s + 1},
+            device_id_type=MESH,
+        )
+
+    def sends(way, d):
+        if way == 0:
+            return jnp.logical_and(s >= d, s < last)
+        return jnp.logical_and(s + d <= last, s > 0)
+
+    def gets(way, d):
+        return s >= d if way == 0 else s + d <= last
+
+    order = sorted(((k, d) for k in range(groups) for d in range(shards)), key=lambda e: (e[0] + e[1], e[0]))
+    for k, d in order:
+        if d == 0 and k:
+            landed = pltpu.make_async_remote_copy(
+                src_ref=half.at[k],
+                dst_ref=out.at[s, lax.rem(t + k, groups)],
+                send_sem=y_send.at[k],
+                recv_sem=y_recv.at[k],
+                device_id={"tensor": lax.rem(t + k, groups)},
+                device_id_type=MESH,
+            )
+            landed.wait_recv()
+        for way in (0, 1):
+            if d:
+                @pl.when(gets(way, d))
+                def _():
+                    arrival(way, k, d).wait_recv()
+            if d < last:
+                @pl.when(sends(way, d))
+                def _():
+                    hop(way, k, d).start()
+        if d == 0 and k == 0:
+            for j in range(1, groups):
+                across(j).start()
+            pltpu.make_async_copy(half.at[0], out.at[s, t], own_sem).start()
+    pltpu.make_async_copy(half.at[0], out.at[s, t], own_sem).wait()
+    for k, d in order:
+        if d == 0 and k:
+            across(k).wait_send()
+        for way in (0, 1):
+            if d < last:
+                @pl.when(sends(way, d))
+                def _():
+                    hop(way, k, d).wait_send()
+
+
+def spread(shards, groups, half):
+    _, rows, cols = half.shape
+    return pl.pallas_call(
+        functools.partial(spread_kernel, shards, groups),
+        out_shape=jax.ShapeDtypeStruct((shards, groups, rows, cols), half.dtype),
+        in_specs=[pl.BlockSpec(memory_space=pl.ANY)],
+        out_specs=pl.BlockSpec(memory_space=pl.ANY),
+        scratch_shapes=[
+            pltpu.SemaphoreType.DMA((groups,)),
+            pltpu.SemaphoreType.DMA((groups,)),
+            pltpu.SemaphoreType.DMA((2, groups, shards)),
+            pltpu.SemaphoreType.DMA((2, groups, shards)),
+            pltpu.SemaphoreType.DMA,
+        ],
+        compiler_params=pltpu.CompilerParams(collective_id=1, has_side_effects=True),
+    )(half)
+
+
 def body(axes, qkv_grad, master, moment_one, moment_two, average, step):
     shards, groups = dict(axes)["shard"], dict(axes)["tensor"]
     t = lax.axis_index("tensor")
@@ -181,15 +245,9 @@
     new_master, new_one, new_two, half = update(
         pos, scal, jnp.stack(pieces), master, moment_one, moment_two
     )
-    weights = None
-    new_average = None
-    for k in range(groups):
-        piece = half[k]
-        if k:
-            piece = lax.ppermute(piece, "tensor", [(i, (i - k) % groups) for i in range(groups)])
-        gathered = lax.all_gather(piece, "shard", axis=0, tiled=False)
-        new_average = average_step(pos, piece, average, groups, k, new_average)
-        weights = place(pos, gathered, groups, k, weights)
+    weights = spread(shards, groups, half)
+    fresh = lax.dynamic_index_in_dim(weights, lax.axis_index("shard"), 0, keepdims=False)
+    new_average = 0.99 * average + 0.01 * fresh.reshape(average.shape).astype(jnp.float32)
     return (weights.reshape(shards * groups * rows, cols), new_master, new_one, new_two, new_average)
 
 

time: 309 us -> 290 us (0.939)
  waiting for transfers between devices: 237 us -> 122 us
  Pallas kernels: 31.4 us -> 124 us
  other arithmetic: 5.88 us -> 9.99 us
    all_gather x2 -> x0, waiting for transfers between devices: 97.1 us -> none  [body(): gathered = lax.all_gather(piece, 'shard', axis=0, tiled=False)]
    pallas_call x4 -> x1, Pallas kernels: 12.2 us -> 105 us  [spread(): pl.pallas_call(functools.partial(spread_kernel, shards, groups), out_shap...]
    ppermute x1 -> x0, waiting for transfers between devices: 18.4 us -> none  [body(): lax.ppermute(piece, 'tensor', [(i, (i - k) % groups) for i in range(group...]
    unnamed x10 -> x15, local copies, waits for them, and re-layouts: 4.91 us -> 7.64 us
  transfers between devices with their start and end apart: 6 -> 3, of which waited for: 5 -> 2; matrix products, arithmetic and copies ran while one was open for 2% -> 2% of each run, Pallas kernels for 7% -> 5%
where the time goes in v3:
time: 290 us
  Pallas kernels  124 us (43%)
  waiting for transfers between devices  122 us (42%)
  between operations  16.9 us (6%)
  local copies, waits for them, and re-layouts  15.4 us (5%)
  other arithmetic  9.99 us (3%)
    reduce_scatter x2, waiting for transfers between devices, body(): lax.psum_scatter(block.reshape(shards * rows, cols), 'shard', scatter_dim...  121 us
    pallas_call x1, Pallas kernels, spread(): pl.pallas_call(functools.partial(spread_kernel, shards, groups), out_shap...  105 us
    pallas_call x1, Pallas kernels, total(): pl.pallas_call(functools.partial(total_kernel, axes), out_shape=jax.Shape...  13.1 us
    unnamed x15, local copies, waits for them, and re-layouts  7.64 us
    pallas_call x1, Pallas kernels, update(): pl.pallas_call(update_kernel, grid_spec=pltpu.PrefetchScalarGridSpec(num_...  6.09 us
    dynamic_slice x1, local copies, waits for them, and re-layouts, body(): lax.dynamic_index_in_dim(blocks, lax.rem(t + k, groups), 1, keepdims=False)  6 us
  transfers between devices with their start and end apart: 3, of which 2 were waited for; matrix products, arithmetic and copies ran while one was open for 2% of the time, Pallas kernels for 5%

profile of v3, /device:TPU:0, one launch (start us, length us, event | category | flops | bytes accessed | tf_op | source)
XLA Modules:
  0.0 289.6 jit_solution(14981542732501280883)
XLA Ops:
  7.2 0.0 reduce-scatter.3.cloned.1.call-start
  7.2 6.0 %constant_dynamic-slice_fusion = (bf16[4,1,128,3072]{3,2,1,0:T(8,128)(2,1)}, bf16[4,1,128,3072]{3,2,1,0:T(8,128)(2,1)}) fusion(bf16[4,2,128,3072]{3,2,1,0:T(8,128)(2,1)} %bitcast.21, s32[]{:T(128)S(6)} %select_n.12, s32[]{:T(128)S(6)} %select_n.11), kind=kLoop, calls=%fused_computation.5 | loop fusion | bytes 12582920 | tf_op jit(solution)/shard_map/jit(dynamic_index_in_dim)/dynamic_slice | solution.py:229
  13.2 0.0 reduce-scatter.3.cloned.1.call-update
  13.3 0.0 reduce-scatter.5.cloned.1.call-start
  13.3 0.7 reduce-scatter.5.cloned.1.call-update
  14.0 0.0 copy-start
  14.0 62.4 %reduce-scatter.3.cloned.1.call-done = bf16[128,3072]{1,0:T(8,128)(2,1)} async-done(((bf16[512,3072]{1,0:T(8,128)(2,1)}), bf16[128,3072]{1,0:T(8,128)(2,1)}) %reduce-scatter.3.cloned.1.call-update) | async-done | bytes 786448 | tf_op jit(solution)/shard_map/reduce_scatter | solution.py:230
  76.4 1.5 collective-permute-start
  78.6 2.1 multiply_reduce_fusion.1
  80.7 58.8 %reduce-scatter.5.cloned.1.call-done = bf16[128,3072]{1,0:T(8,128)(2,1)} async-done(((bf16[512,3072]{1,0:T(8,128)(2,1)}), bf16[128,3072]{1,0:T(8,128)(2,1)}) %reduce-scatter.5.cloned.1.call-update) | async-done | bytes 786448 | tf_op jit(solution)/shard_map/reduce_scatter | solution.py:230
  139.5 2.1 multiply_reduce_fusion
  143.0 0.6 broadcast_in_dim.3.x_ref
  143.6 13.1 %shard_map.101 = f32[8,128]{1,0:T(8,128)} custom-call(f32[8,128]{1,0:T(8,128)} %broadcast_in_dim.3.x_ref), custom_call_target="tpu_custom_call" | custom-call | tf_op jit(solution)/shard_map/pallas_call | solution.py:88
  156.7 1.2 slice.3
  158.6 0.1 pad_maximum_fusion.1.scal
  158.7 0.0 collective-permute-done
  158.7 1.5 pad_maximum_fusion.grad
  160.2 0.0 copy-done
  160.2 0.0 copy-start.1
  160.2 1.9 copy-done.1
  162.1 1.9 copy-done.2
  164.0 6.1 %shard_map.102 = (f32[128,6144]{1,0:T(8,128)}, f32[128,6144]{1,0:T(8,128)}, f32[128,6144]{1,0:T(8,128)}, bf16[2,128,3072]{2,1,0:T(8,128)(2,1)S(1)}) custom-call(s32[1]{0:T(128)} %bitcast.pos, f32[3]{0:T(128)S(1)} %pad_maximum_fusion.1.scal, bf16[2,128,3072]{2,1,0:T(8,128)(2,1)S(1)} %pad_maximum_fusion.grad, f32[128,6144]{1,0:T(8,128)S(1)} %copy-done, ...), custom_call_target="tpu_custom_call" | custom-call | flops 12582912 | bytes 22020096 | tf_op jit(solution)/shard_map/pallas_call | solution.py:33
  170.1 1.1 copy-done.3
  171.2 104.7 %shard_map.103 = bf16[4,2,128,3072]{3,2,1,0:T(8,128)(2,1)} custom-call(bf16[2,128,3072]{2,1,0:T(8,128)(2,1)} %copy-done.3), custom_call_target="tpu_custom_call" | custom-call | tf_op jit(solution)/shard_map/pallas_call | solution.py:203
  275.9 0.0 slice-start
  275.9 1.9 convert_multiply_fusion
  277.8 0.0 copy-done.4
  277.8 0.0 slice-start.1
  277.9 2.2 bitcast_add_fusion
  280.0 0.0 slice-done
  280.0 0.0 slice-done.1
  280.0 2.7 copy.17
  (4 shorter events, 0.0 us)
Async XLA Ops:
  7.2 69.2 %reduce-scatter.3.cloned.1.call-start = ((), (), s32[]{:S(2)}) async-start(), calls=%async_computation.2 | async-start | bytes 3932160 | tf_op jit(solution)/shard_map/reduce_scatter | solution.py:230
  13.3 126.3 %reduce-scatter.5.cloned.1.call-start = ((), (), s32[]{:S(2)}) async-start(), calls=%async_computation.3 | async-start | bytes 3932160 | tf_op jit(solution)/shard_map/reduce_scatter | solution.py:230
  14.0 146.2 %copy-start = (f32[128,6144]{1,0:T(8,128)S(1)}, f32[128,6144]{1,0:T(8,128)}, u32[]{:S(2)}) copy-start(f32[128,6144]{1,0:T(8,128)} %master.1) | copy-start | bytes 9437188
  76.4 82.3 %collective-permute-start = (bf16[128,3072]{1,0:T(8,128)(2,1)}, bf16[128,3072]{1,0:T(8,128)(2,1)}, u32[]{:S(2)}, u32[]{:S(2)}) collective-permute-start(bf16[128,3072]{1,0:T(8,128)(2,1)} %reduce-scatter.3.cloned.1.call-done), channel_id=1, source_target_pairs={{0,4},{4,0},{1,5},{5,1},{2,6},{6,2},{3,7},{7,3},{8,12},{12,8},{9,1... | collective-permute-start | bytes 2359304 | tf_op jit(solution)/shard_map/ppermute | solution.py:236
  160.2 1.9 copy-start.1
  162.1 1.9 copy-start.2
  170.1 1.1 copy-start.3
  171.2 106.6 %copy-start.4 = (f32[256,3072]{1,0:T(8,128)S(1)}, f32[256,3072]{1,0:T(8,128)}, u32[]{:S(2)}) copy-start(f32[256,3072]{1,0:T(8,128)} %param.10) | copy-start | bytes 9437188
  275.9 4.1 %slice-start = ((s8[6291456]{0:T(1024)(128)(4,1)}), s8[4194304]{0:T(1024)(128)(4,1)S(1)}, s32[]{:S(2)}) async-start(s8[6291456]{0:T(1024)(128)(4,1)} %bitcast.16), calls=%async_computation.4 | async-start | bytes 8388608
  277.8 2.2 slice-start.1
Sparse Core Ops, SparseCore 0:
  13.4 62.9 reduce-scatter.2
  79.3 60.2 reduce-scatter.4

commit v4 on v3

--- a/solution.py
+++ b/solution.py
@@ -216,6 +216,154 @@
     )(half)
 
 
+def reduce_kernel(shards, groups, x, out, square, inbox, own, ybox, z_send, z_recv, y_send, y_recv):
+    s = lax.axis_index("shard")
+    t = lax.axis_index("tensor")
+    last = shards - 1
+    rows = x.shape[2]
+    tile = min(rows, 16)
+    barrier = pltpu.get_barrier_semaphore()
+    for off in range(1, groups):
+        pl.semaphore_signal(
+            barrier, inc=1, device_id={"tensor": lax.rem(t + off, groups)}, device_id_type=MESH
+        )
+
+    @pl.when(s < last)
+    def _():
+        pl.semaphore_signal(barrier, inc=1, device_id={"shard": s + 1}, device_id_type=MESH)
+
+    @pl.when(s > 0)
+    def _():
+        pl.semaphore_signal(barrier, inc=1, device_id={"shard": s - 1}, device_id_type=MESH)
+
+    peers = groups - 1 + jnp.minimum(s, 1) + jnp.minimum(last - s, 1)
+    pl.semaphore_wait(barrier, peers)
+    square[...] = jnp.zeros_like(square)
+
+    def hop(way, k, q, first):
+        return pltpu.make_async_remote_copy(
+            src_ref=x.at[q, lax.rem(t + k, groups)] if first else inbox.at[way, k, q],
+            dst_ref=inbox.at[way, k, q],
+            send_sem=z_send.at[way, k, q],
+            recv_sem=z_recv.at[way, k, q],
+            device_id={"shard": s + 1 if way == 0 else s - 1},
+            device_id_type=MESH,
+        )
+
+    def arrival(way, k, q):
+        return pltpu.make_async_remote_copy(
+            src_ref=inbox.at[way, k, q],
+            dst_ref=inbox.at[way, k, q],
+            send_sem=z_send.at[way, k, q],
+            recv_sem=z_recv.at[way, k, q],
+            device_id={"shard": s - 1 if way == 0 else s + 1},
+            device_id_type=MESH,
+        )
+
+    def roles(way, q):
+        if way == 0:
+            return jnp.logical_and(s == 0, q > 0), jnp.logical_and(s > 0, s < q)
+        return jnp.logical_and(s == last, q < last), jnp.logical_and(s < last, s > q)
+
+    def forward(way, k, q):
+        first, middle = roles(way, q)
+        group = lax.rem(t + k, groups)
+
+        @pl.when(first)
+        def _():
+            hop(way, k, q, True).start()
+
+        @pl.when(middle)
+        def _():
+            arrival(way, k, q).wait_recv()
+
+            @pl.loop(0, rows // tile)
+            def _(i):
+                part = pl.ds(pl.multiple_of(i * tile, tile), tile)
+                both = inbox[way, k, q, part].astype(jnp.float32) + x[q, group, part].astype(jnp.float32)
+                inbox[way, k, q, part] = both.astype(jnp.bfloat16)
+
+            hop(way, k, q, False).start()
+
+    def across(k):
+        return pltpu.make_async_remote_copy(
+            src_ref=own.at[k],
+            dst_ref=ybox.at[k],
+            send_sem=y_send.at[k],
+            recv_sem=y_recv.at[k],
+            device_id={"tensor": lax.rem(t + k, groups)},
+            device_id_type=MESH,
+        )
+
+    def finish(k):
+        group = lax.rem(t + k, groups)
+        for q in range(shards):
+            @pl.when(s == q)
+            def _():
+                ways = [way for way in (0, 1) if (q > 0 if way == 0 else q < last)]
+                for way in ways:
+                    arrival(way, k, q).wait_recv()
+
+                @pl.loop(0, rows // tile)
+                def _(i):
+                    part = pl.ds(pl.multiple_of(i * tile, tile), tile)
+                    acc = x[q, group, part].astype(jnp.float32)
+                    for way in ways:
+                        acc = acc + inbox[way, k, q, part].astype(jnp.float32)
+                    own[k, part] = acc.astype(jnp.bfloat16)
+                    square[...] += jnp.sum((acc * acc).reshape(tile // 8, 8, acc.shape[1]), axis=0)
+
+        if k:
+            across(k).start()
+
+    pairs = [(way, j) for j in range(last) for way in (0, 1)]
+    for k in range(groups - 1, -1, -1):
+        for n, (way, j) in enumerate(pairs):
+            forward(way, k, last - j if way == 0 else j)
+            if n == 1 and k < groups - 1:
+                finish(k + 1)
+    finish(0)
+    out[0] = own[0]
+    for k in range(1, groups):
+        across(k).wait_recv()
+        out[k] = ybox[k]
+        across(k).wait_send()
+    for k in range(groups):
+        for way in (0, 1):
+            for q in range(shards):
+                first, middle = roles(way, q)
+
+                @pl.when(jnp.logical_or(first, middle))
+                def _():
+                    hop(way, k, q, False).wait_send()
+
+
+def reduce_shares(shards, groups, x):
+    _, _, rows, cols = x.shape
+    whole = pl.BlockSpec(memory_space=pltpu.VMEM)
+    return pl.pallas_call(
+        functools.partial(reduce_kernel, shards, groups),
+        out_shape=[
+            jax.ShapeDtypeStruct((groups, rows, cols), jnp.bfloat16),
+            jax.ShapeDtypeStruct((8, cols), jnp.float32),
+        ],
+        in_specs=[whole],
+        out_specs=[whole, whole],
+        scratch_shapes=[
+            pltpu.VMEM((2, groups, shards, rows, cols), jnp.bfloat16),
+            pltpu.VMEM((groups, rows, cols), jnp.bfloat16),
+            pltpu.VMEM((groups, rows, cols), jnp.bfloat16),
+            pltpu.SemaphoreType.DMA((2, groups, shards)),
+            pltpu.SemaphoreType.DMA((2, groups, shards)),
+            pltpu.SemaphoreType.DMA((groups,)),
+            pltpu.SemaphoreType.DMA((groups,)),
+        ],
+        compiler_params=pltpu.CompilerParams(
+            collective_id=2, has_side_effects=True, vmem_limit_bytes=48 * 2**20
+        ),
+    )(x)
+
+
 def body(axes, qkv_grad, master, moment_one, moment_two, average, step):
     shards, groups = dict(axes)["shard"], dict(axes)["tensor"]
     t = lax.axis_index("tensor")
@@ -223,18 +371,8 @@
     rows = qkv_grad.shape[1] // (shards * groups)
     cols = qkv_grad.shape[2]
     blocks = qkv_grad.reshape(shards, groups, rows, cols)
-    pieces = [None] * groups
-    local_sq = jnp.float32(0.0)
-    for k in range(groups - 1, -1, -1):
-        block = lax.dynamic_index_in_dim(blocks, lax.rem(t + k, groups), 1, keepdims=False)
-        share = lax.psum_scatter(
-            block.reshape(shards * rows, cols), "shard", scatter_dimension=0, tiled=True
-        )
-        wide = share.astype(jnp.float32)
-        local_sq = local_sq + jnp.sum(wide * wide)
-        if k:
-            share = lax.ppermute(share, "tensor", [(i, (i + k) % groups) for i in range(groups)])
-        pieces[k] = share
+    pieces, square = reduce_shares(shards, groups, blocks)
+    local_sq = jnp.sum(square)
     sumsq = total(axes, local_sq)
     limit = jnp.float32(math.sqrt(D * QKV))
     clip = jnp.minimum(jnp.float32(1.0), limit / (jnp.sqrt(sumsq) + 1e-06))
@@ -243,7 +381,7 @@
     second_fix = 1.0 - jnp.power(jnp.float32(0.95), count)
     scal = jnp.stack([clip, first_fix, second_fix])
     new_master, new_one, new_two, half = update(
-        pos, scal, jnp.stack(pieces), master, moment_one, moment_two
+        pos, scal, pieces, master, moment_one, moment_two
     )
     weights = spread(shards, groups, half)
     fresh = lax.dynamic_index_in_dim(weights, lax.axis_index("shard"), 0, keepdims=False)

time: 290 us -> 270 us (0.931)
  Pallas kernels: 124 us -> 249 us
  waiting for transfers between devices: 122 us -> 0 us
  between operations: 16.9 us -> 2.17 us
  other arithmetic: 9.99 us -> 4.97 us
    pallas_call x0 -> x1, Pallas kernels: none -> 125 us  [reduce_shares(): pl.pallas_call(functools.partial(reduce_kernel, shards, groups), out_shap...]
    reduce_scatter x2 -> x0, waiting for transfers between devices: 121 us -> none  [body(): lax.psum_scatter(block.reshape(shards * rows, cols), 'shard', scatter_dim...]
    dynamic_slice x1 -> x0, local copies, waits for them, and re-layouts: 6 us -> none  [body(): lax.dynamic_index_in_dim(blocks, lax.rem(t + k, groups), 1, keepdims=False)]
    reduce_sum x2 -> x1, other arithmetic: 4.29 us -> 0.65 us  [body(): local_sq = jnp.sum(square)]
    unnamed x15 -> x19, local copies, waits for them, and re-layouts: 7.64 us -> 10.8 us
  transfers between devices with their start and end apart: 3 -> 0, of which waited for: 2 -> 0; matrix products, arithmetic and copies ran while one was open for 2% -> 0% of each run, Pallas kernels for 5% -> 0%
where the time goes in v4:
time: 270 us
  Pallas kernels  249 us (92%)
  local copies, waits for them, and re-layouts  13.2 us (5%)
  other arithmetic  4.97 us (2%)
    pallas_call x1, Pallas kernels, reduce_shares(): pl.pallas_call(functools.partial(reduce_kernel, shards, groups), out_shap...  125 us
    pallas_call x1, Pallas kernels, spread(): pl.pallas_call(functools.partial(spread_kernel, shards, groups), out_shap...  104 us
    pallas_call x1, Pallas kernels, total(): pl.pallas_call(functools.partial(total_kernel, axes), out_shape=jax.Shape...  14.1 us
    unnamed x19, local copies, waits for them, and re-layouts  10.8 us
    pallas_call x1, Pallas kernels, update(): pl.pallas_call(update_kernel, grid_spec=pltpu.PrefetchScalarGridSpec(num_...  6.09 us

profile of v4, /device:TPU:0, one launch (start us, length us, event | category | flops | bytes accessed | tf_op | source)
XLA Modules:
  0.0 269.6 jit_solution(9308494035919666093)
XLA Ops:
  1.4 0.0 copy-start
  1.4 125.3 %shard_map.101 = (bf16[2,128,3072]{2,1,0:T(8,128)(2,1)S(1)}, f32[8,3072]{1,0:T(8,128)S(1)}) custom-call(bf16[4,2,128,3072]{3,2,1,0:T(8,128)(2,1)} %bitcast.11), custom_call_target="tpu_custom_call" | custom-call | tf_op jit(solution)/shard_map/pallas_call | solution.py:344
  126.7 0.0 copy-start.3
  126.7 1.1 copy-done.3
  127.8 0.6 reduce_sum.9
  128.5 1.2 broadcast_in_dim.3.x_ref
  129.7 14.1 %shard_map.102 = f32[8,128]{1,0:T(8,128)} custom-call(f32[8,128]{1,0:T(8,128)} %broadcast_in_dim.3.x_ref), custom_call_target="tpu_custom_call" | custom-call | tf_op jit(solution)/shard_map/pallas_call | solution.py:88
  143.8 1.2 slice.3
  145.7 0.1 pad_maximum_fusion.scal
  145.8 0.0 copy-done
  145.8 0.0 copy-start.1
  145.8 1.9 copy-done.1
  147.7 0.0 copy-start.2
  147.7 1.9 copy-done.2
  149.6 0.0 copy-start.4
  149.6 1.4 copy-done.4
  151.0 6.1 %shard_map.103 = (f32[128,6144]{1,0:T(8,128)}, f32[128,6144]{1,0:T(8,128)}, f32[128,6144]{1,0:T(8,128)}, bf16[2,128,3072]{2,1,0:T(8,128)(2,1)S(1)}) custom-call(s32[1]{0:T(128)} %bitcast.pos, f32[3]{0:T(128)S(1)} %pad_maximum_fusion.scal, bf16[2,128,3072]{2,1,0:T(8,128)(2,1)S(1)} %copy-done.4, f32[128,6144]{1,0:T(8,128)S(1)} %copy-done, ...), custom_call_target="tpu_custom_call" | custom-call | flops 12582912 | bytes 22020096 | tf_op jit(solution)/shard_map/pallas_call | solution.py:33
  157.1 0.0 copy-start.5
  157.1 1.1 copy-done.5
  158.2 103.8 %shard_map.104 = bf16[4,2,128,3072]{3,2,1,0:T(8,128)(2,1)} custom-call(bf16[2,128,3072]{2,1,0:T(8,128)(2,1)} %copy-done.5), custom_call_target="tpu_custom_call" | custom-call | tf_op jit(solution)/shard_map/pallas_call | solution.py:203
  262.0 0.0 copy-start.6
  262.0 0.0 slice-start
  262.0 1.9 convert_multiply_fusion
  263.9 0.4 copy-done.6
  264.4 0.0 slice-start.1
  264.4 2.3 bitcast_add_fusion
  266.7 0.0 slice-done
  266.7 0.2 slice-done.1
  266.9 2.7 %copy.13 = bf16[1024,3072]{1,0:T(8,128)(2,1)} copy(bf16[1024,3072]{1,0:T(8,128)(2,1)S(1)} %bitcast.10) | data formatting | bytes 12582912
  (1 shorter events, 0.0 us)
Async XLA Ops:
  1.4 144.4 %copy-start = (f32[128,6144]{1,0:T(8,128)S(1)}, f32[128,6144]{1,0:T(8,128)}, u32[]{:S(2)}) copy-start(f32[128,6144]{1,0:T(8,128)} %master.1) | copy-start | bytes 9437188
  126.7 1.1 copy-start.3
  145.8 1.9 copy-start.1
  147.7 1.9 copy-start.2
  149.6 1.4 copy-start.4
  157.1 1.1 copy-start.5
  262.0 2.4 copy-start.6
  262.0 4.7 %slice-start = ((s8[6291456]{0:T(1024)(128)(4,1)}), s8[4194304]{0:T(1024)(128)(4,1)S(1)}, s32[]{:S(2)}) async-start(s8[6291456]{0:T(1024)(128)(4,1)} %bitcast.8), calls=%async_computation | async-start | bytes 8388608
  264.4 2.5 slice-start.1
